TPU v7x, 32 devices: a whole 2x2x4 slice. The times are simulated.
32 devices in a mesh: box: 4 (over y, x), col: 8 (over z, core).
Axes of the slice: x: 2, y: 2, z: 4, core: 2. Of those that a mesh axis runs over, the one named last changes fastest.
Arguments:
- box_maps: bfloat16 [4, 2, 1024, 2048], P('box', None, 'col'), may hold values from -1 to 1
- group_loads: float32 [4, 128, 2048], P('box', 'col'), may hold values from -6 to 6
Outputs:
- top_maps: float32 [4, 2, 1024, 512], P('box', None, 'col')
- leaf_data: float32 [4, 512, 2048], P('box', 'col')
All inputs are finite; a program needn't handle non-finite values.
Results may differ from a plain program's by a relative error of at most 0.0076.
Values may be sent and summed in bfloat16 or wider, within the bound.
No kernel may reach another device: no remote copies, remote signals or barrier semaphores. Data moves between devices by JAX's collectives and lax.ppermute only.
A program may use at most 192 MiB of HBM per device.

v0:
```python
import jax
import jax.numpy as jnp
from jax import lax
from jax.sharding import PartitionSpec as P


def partner_2(value, axis, distance):
    mask = 2**distance
    pairs = [(source, source ^ mask) for source in range(lax.axis_size(axis))]
    return lax.ppermute(value, axis, pairs)


def rows_by_rows(left_rows, right_rows):
    return lax.dot_general(
        left_rows,
        right_rows,
        (((1,), (1,)), ((), ())),
        precision=lax.Precision.HIGHEST,
        preferred_element_type=jnp.float32,
    )


def factor_interface(left_faces, right_faces):
    middle = left_faces.shape[0]
    share = middle // lax.axis_size("col")
    product = jnp.dot(
        right_faces[:, middle:], left_faces[:, middle:], preferred_element_type=jnp.float32
    )
    coupling = jnp.eye(middle, dtype=jnp.float32) - product
    row_start = lax.axis_index("col") * share
    own_rows = lax.dynamic_slice_in_dim(coupling, row_start, share, 0)
    own_gram = rows_by_rows(own_rows, coupling)
    gram = lax.all_gather(own_gram, "col", axis=0, tiled=True)
    return (coupling, jnp.linalg.cholesky(gram))


def apply_inverse(incoming, coupling, triangle):
    moved = rows_by_rows(incoming, coupling)
    return jax.scipy.linalg.cho_solve((triangle, True), moved.T).T


def exchange_children(own_block, bit_number):
    middle = own_block.shape[2] // 2
    is_left = lax.axis_index("box") // (1 << bit_number) % 2 == 0
    partner = partner_2(own_block, "box", bit_number)
    left_block = jnp.where(is_left, own_block, partner)
    right_block = jnp.where(is_left, partner, own_block)
    left_faces, right_faces, left_cross, right_cross = (
        lax.all_gather(left_block[1], "col", axis=0, tiled=True),
        lax.all_gather(right_block[1], "col", axis=0, tiled=True),
        lax.all_gather(left_block[0][:, middle:], "col", axis=0, tiled=True),
        lax.all_gather(right_block[0][:, middle:], "col", axis=0, tiled=True),
    )
    return (left_block, right_block, left_faces, right_faces, left_cross, right_cross)


def merge_columns(
    left_outer, right_outer, left_faces, right_faces, coupling, triangle, offset, extent
):
    middle = left_faces.shape[0]
    own_count = left_outer.shape[0]
    left_top = lax.dynamic_slice_in_dim(left_faces, offset, extent, 1)
    right_top = lax.dynamic_slice_in_dim(right_faces, offset, extent, 1)
    left_inner = left_faces[:, middle:]
    right_inner = right_faces[:, middle:]
    driven = jnp.dot(right_outer[:, middle:], left_inner, preferred_element_type=jnp.float32)
    both_solved = apply_inverse(
        jnp.concatenate([left_outer[:, middle:].astype(jnp.float32), driven], axis=0),
        coupling,
        triangle,
    ).astype(jnp.bfloat16)
    solved_left = both_solved[:own_count]
    solved_right = both_solved[own_count:]
    carried_left = jnp.dot(solved_left, right_inner, preferred_element_type=jnp.float32)
    upper_left = lax.dynamic_slice_in_dim(left_outer, offset, extent, 1).astype(
        jnp.float32
    ) + jnp.dot(carried_left.astype(jnp.bfloat16), left_top, preferred_element_type=jnp.float32)
    lower_left = jnp.dot(solved_left, right_top, preferred_element_type=jnp.float32)
    carried_right = right_outer[:, middle:].astype(jnp.float32) + jnp.dot(
        solved_right, right_inner, preferred_element_type=jnp.float32
    )
    upper_right = jnp.dot(
        carried_right.astype(jnp.bfloat16), left_top, preferred_element_type=jnp.float32
    )
    lower_right = lax.dynamic_slice_in_dim(right_outer, offset, extent, 1).astype(
        jnp.float32
    ) + jnp.dot(solved_right, right_top, preferred_element_type=jnp.float32)
    return (upper_left, lower_left, upper_right, lower_right)


def solve_down(incoming, operators, coupling, triangle):
    left_faces = operators[2]
    right_faces = operators[3]
    left_cross = operators[4]
    right_cross = operators[5]
    middle = left_faces.shape[0]
    given_left = incoming[:, :middle]
    given_right = incoming[:, middle:]
    through = jnp.dot(
        given_right.astype(jnp.bfloat16), right_cross, preferred_element_type=jnp.float32
    )
    driven = jnp.dot(
        given_left.astype(jnp.bfloat16), left_cross, preferred_element_type=jnp.float32
    ) + jnp.dot(
        through.astype(jnp.bfloat16), left_faces[:, middle:], preferred_element_type=jnp.float32
    )
    solved_left = apply_inverse(driven, coupling, triangle)
    solved_right = through + jnp.dot(
        solved_left.astype(jnp.bfloat16),
        right_faces[:, middle:],
        preferred_element_type=jnp.float32,
    )
    return (
        jnp.concatenate([given_left, solved_right], axis=1),
        jnp.concatenate([given_right, solved_left], axis=1),
    )


def per_device(box_maps, group_loads):
    own_block = box_maps[0]
    port_count = own_block.shape[2]
    middle = port_count // 2
    quarter = port_count // 4
    level_one = exchange_children(own_block, 0)
    coupling_one, triangle_one = factor_interface(level_one[2], level_one[3])
    piece_list = merge_columns(
        level_one[0][0],
        level_one[1][0],
        level_one[2],
        level_one[3],
        coupling_one,
        triangle_one,
        0,
        middle,
    )
    pair_block = jnp.stack(
        [
            jnp.concatenate([piece_list[0], piece_list[1]], axis=1),
            jnp.concatenate([piece_list[2], piece_list[3]], axis=1),
        ]
    ).astype(jnp.bfloat16)
    second = exchange_children(pair_block, 1)
    coupling_two, triangle_two = factor_interface(second[2], second[3])
    position = lax.axis_index("box") % 4
    offset = position % 2 * quarter
    part_list = merge_columns(
        second[0][0],
        second[1][0],
        second[2],
        second[3],
        coupling_two,
        triangle_two,
        offset,
        quarter,
    )
    upper_side = position < 2
    top_block = jnp.stack(
        [
            jnp.where(upper_side, part_list[0], part_list[1]),
            jnp.where(upper_side, part_list[2], part_list[3]),
        ]
    )
    rows_top = group_loads[0]
    count_rows = rows_top.shape[0]
    bit_zero = lax.axis_index("box") % 2 == 0
    bit_one = lax.axis_index("box") // 2 % 2 == 0
    received = partner_2(rows_top.astype(jnp.bfloat16), "box", 0).astype(rows_top.dtype)
    pair_set = jnp.stack(
        [jnp.where(bit_zero, rows_top, received), jnp.where(bit_zero, received, rows_top)]
    )
    received_set = partner_2(pair_set.astype(jnp.bfloat16), "box", 1).astype(pair_set.dtype)
    all_rows = jnp.stack(
        [jnp.where(bit_one, pair_set, received_set), jnp.where(bit_one, received_set, pair_set)]
    ).reshape(4 * count_rows, port_count)
    pair_left, pair_right = solve_down(all_rows, second, coupling_two, triangle_two)
    pair_rows = jnp.where(bit_one, pair_left, pair_right)
    box_left, box_right = solve_down(pair_rows, level_one, coupling_one, triangle_one)
    leaf_block = jnp.where(bit_zero, box_left, box_right)
    return (top_block[None], leaf_block[None])


def solution(mesh):
    placed = (P("box", None, "col", None), P("box", "col", None))
    return jax.shard_map(
        per_device,
        mesh=mesh,
        in_specs=placed,
        out_specs=(P("box", None, "col", None), P("box", "col", None)),
        check_vma=False,
    )
```

profile of v0, /device:TPU:0, one launch (start us, length us, event | category | flops | bytes accessed | tf_op | source)
XLA Modules:
  0.0 1155.9 jit_solution(14508140879100234056)
XLA Ops:
  10.2 23.4 %collective-permute-done = bf16[2,128,2048]{2,1,0:T(8,128)(2,1)S(1)} collective-permute-done((bf16[2,128,2048]{2,1,0:T(8,128)(2,1)}, bf16[2,128,2048]{2,1,0:T(8,128)(2,1)S(1)}, u32[]{:S(2)}, u32[]{:S(2)}) %collective-permute-start) | collective-permute-done | bytes 1048608 | tf_op jit(solution)/shard_map/ppermute | solution.py:10
  36.9 47.5 %all-gather.27.cloned.1.call-done = bf16[1,1024,2048]{2,1,0:T(8,128)(2,1)} async-done(((bf16[1,128,2048]{2,1,0:T(8,128)(2,1)}), bf16[1,1024,2048]{2,1,0:T(8,128)(2,1)}) %all-gather.27.cloned.1.call-update) | async-done | bytes 4194320 | tf_op jit(solution)/shard_map/all_gather | solution.py:50
  84.4 47.9 %all-gather.29.cloned.1.call-done = bf16[1,1024,2048]{2,1,0:T(8,128)(2,1)} async-done(((bf16[1,128,2048]{2,1,0:T(8,128)(2,1)}), bf16[1,1024,2048]{2,1,0:T(8,128)(2,1)}) %all-gather.29.cloned.1.call-update) | async-done | bytes 4194320 | tf_op jit(solution)/shard_map/all_gather | solution.py:49
  149.9 39.9 %all-gather.15.cloned.1.call-done = f32[1024,1024]{0,1:T(8,128)} async-done(((f32[128,1024]{0,1:T(8,128)}), f32[1024,1024]{0,1:T(8,128)}) %all-gather.15.cloned.1.call-update) | async-done | bytes 4194320 | tf_op jit(solution)/shard_map/all_gather | solution.py:33
  189.8 5.8 copy.5
  202.0 11.7 %cholesky.619 = f32[128,128]{1,0:T(8,128)S(1)} custom-call(f32[128,128]{1,0:T(8,128)S(1)} %cholesky.911), custom_call_target="Cholesky" | custom-call | tf_op jit(solution)/shard_map/jit(cholesky)/cholesky | solution.py:34
  216.2 9.8 custom-call.63
  229.9 11.9 %cholesky.638 = f32[128,128]{1,0:T(8,128)S(1)} custom-call(f32[128,128]{1,0:T(8,128)S(1)} %cholesky.915), custom_call_target="Cholesky" | custom-call | tf_op jit(solution)/shard_map/jit(cholesky)/cholesky | solution.py:34
  242.5 9.8 custom-call.64
  255.6 11.7 %cholesky.659 = f32[128,128]{1,0:T(8,128)S(1)} custom-call(f32[128,128]{1,0:T(8,128)S(1)} %cholesky.920), custom_call_target="Cholesky" | custom-call | tf_op jit(solution)/shard_map/jit(cholesky)/cholesky | solution.py:34
  268.0 9.8 custom-call.65
  281.3 11.9 %cholesky.678 = f32[128,128]{1,0:T(8,128)S(1)} custom-call(f32[128,128]{1,0:T(8,128)S(1)} %cholesky.925), custom_call_target="Cholesky" | custom-call | tf_op jit(solution)/shard_map/jit(cholesky)/cholesky | solution.py:34
  293.9 9.8 custom-call.66
  307.1 11.7 %cholesky.697 = f32[128,128]{1,0:T(8,128)S(1)} custom-call(f32[128,128]{1,0:T(8,128)S(1)} %cholesky.930), custom_call_target="Cholesky" | custom-call | tf_op jit(solution)/shard_map/jit(cholesky)/cholesky | solution.py:34
  319.5 10.2 custom-call.67
  333.0 11.7 %cholesky.716 = f32[128,128]{1,0:T(8,128)S(1)} custom-call(f32[128,128]{1,0:T(8,128)S(1)} %cholesky.935), custom_call_target="Cholesky" | custom-call | tf_op jit(solution)/shard_map/jit(cholesky)/cholesky | solution.py:34
  345.3 9.8 custom-call.68
  358.1 11.7 %cholesky.735 = f32[128,128]{1,0:T(8,128)S(1)} custom-call(f32[128,128]{1,0:T(8,128)S(1)} %cholesky.940), custom_call_target="Cholesky" | custom-call | tf_op jit(solution)/shard_map/jit(cholesky)/cholesky | solution.py:34
  370.5 9.8 custom-call.69
  383.0 11.7 %cholesky.752 = f32[128,128]{1,0:T(8,128)S(1)} custom-call(f32[128,128]{1,0:T(8,128)S(1)} %convolution_subtract_fusion.41), custom_call_target="Cholesky" | custom-call | tf_op jit(solution)/shard_map/jit(cholesky)/cholesky | solution.py:34
  405.0 4.8 select_select_fusion.1
  409.8 23.2 %while.8 = (s32[]{:T(128)}, f32[1024,1024]{1,0:T(8,128)}, s32[8,2]{0,1:T(2,128)S(1)}, f32[8,128,128]{2,1,0:T(8,128)S(1)}, s32[]{:T(128)}) while((s32[]{:T(128)}, f32[1024,1024]{1,0:T(8,128)}, s32[8,2]{0,1:T(2,128)S(1)}, f32[8,128,128]{2,1,0:T(8,128)S(1)}, s32[]{:T(128)}) %tuple.179), condition=%wide.while_cond, body=%wide.while_body.sunk | while | flops 2 | bytes 131189 | solution.py:39
  433.0 78.8 %custom-call.70 = f32[8,128,128]{1,2,0:T(8,128)S(1)} custom-call(f32[8,128,128]{2,1,0:T(8,128)S(1)} %get-tuple-element.33), custom_call_target="InvertDiagBlocksLowerTriangular" | custom-call | tf_op jit(solution)/shard_map/jit(_cho_solve)/triangular_solve | solution.py:39
  538.2 23.9 %collective-permute-done.1 = bf16[2,128,2048]{2,1,0:T(8,128)(2,1)} collective-permute-done((bf16[2,128,2048]{2,1,0:T(8,128)(2,1)S(1)}, bf16[2,128,2048]{2,1,0:T(8,128)(2,1)}, u32[]{:S(2)}, u32[]{:S(2)}) %collective-permute-start.1) | collective-permute-done | bytes 1048608 | tf_op jit(solution)/shard_map/ppermute | solution.py:10
  567.8 42.1 %all-gather.33.cloned.1.call-done = bf16[1,1024,2048]{2,1,0:T(8,128)(2,1)} async-done(((bf16[1,128,2048]{2,1,0:T(8,128)(2,1)}), bf16[1,1024,2048]{2,1,0:T(8,128)(2,1)}) %all-gather.33.cloned.1.call-update) | async-done | bytes 4194320 | tf_op jit(solution)/shard_map/all_gather | solution.py:49
  609.9 47.2 %all-gather.31.cloned.1.call-done = bf16[1,1024,2048]{2,1,0:T(8,128)(2,1)} async-done(((bf16[1,128,2048]{2,1,0:T(8,128)(2,1)}), bf16[1,1024,2048]{2,1,0:T(8,128)(2,1)}) %all-gather.31.cloned.1.call-update) | async-done | bytes 4194320 | tf_op jit(solution)/shard_map/all_gather | solution.py:50
  679.2 7.3 all-gather.19.cloned.1.call-done
  688.6 28.1 %all-gather.21.cloned.1.call-done = bf16[1024,1024]{1,0:T(8,128)(2,1)} async-done(((bf16[128,1024]{1,0:T(8,128)(2,1)}), bf16[1024,1024]{1,0:T(8,128)(2,1)}) %all-gather.21.cloned.1.call-update) | async-done | bytes 2097168 | tf_op jit(solution)/shard_map/all_gather | solution.py:51
  730.8 35.3 %all-gather.17.cloned.1.call-done = f32[1024,1024]{0,1:T(8,128)} async-done(((f32[128,1024]{0,1:T(8,128)}), f32[1024,1024]{0,1:T(8,128)}) %all-gather.17.cloned.1.call-update) | async-done | bytes 4194320 | tf_op jit(solution)/shard_map/all_gather | solution.py:33
  766.1 5.6 copy.7
  778.4 11.7 %cholesky.767 = f32[128,128]{1,0:T(8,128)S(1)} custom-call(f32[128,128]{1,0:T(8,128)S(1)} %cholesky.944), custom_call_target="Cholesky" | custom-call | tf_op jit(solution)/shard_map/jit(cholesky)/cholesky | solution.py:34
  792.6 9.8 custom-call.71
  807.2 12.1 %cholesky.786 = f32[128,128]{1,0:T(8,128)S(1)} custom-call(f32[128,128]{1,0:T(8,128)S(1)} %cholesky.948), custom_call_target="Cholesky" | custom-call | tf_op jit(solution)/shard_map/jit(cholesky)/cholesky | solution.py:34
  819.9 9.8 custom-call.72
  834.1 11.7 %cholesky.807 = f32[128,128]{1,0:T(8,128)S(1)} custom-call(f32[128,128]{1,0:T(8,128)S(1)} %cholesky.953), custom_call_target="Cholesky" | custom-call | tf_op jit(solution)/shard_map/jit(cholesky)/cholesky | solution.py:34
  846.4 9.8 custom-call.73
  859.8 11.9 %cholesky.826 = f32[128,128]{1,0:T(8,128)S(1)} custom-call(f32[128,128]{1,0:T(8,128)S(1)} %cholesky.958), custom_call_target="Cholesky" | custom-call | tf_op jit(solution)/shard_map/jit(cholesky)/cholesky | solution.py:34
  872.3 9.8 custom-call.74
  885.6 11.7 %cholesky.845 = f32[128,128]{1,0:T(8,128)S(1)} custom-call(f32[128,128]{1,0:T(8,128)S(1)} %cholesky.963), custom_call_target="Cholesky" | custom-call | tf_op jit(solution)/shard_map/jit(cholesky)/cholesky | solution.py:34
  897.9 10.0 custom-call.75
  911.3 11.7 %cholesky.864 = f32[128,128]{1,0:T(8,128)S(1)} custom-call(f32[128,128]{1,0:T(8,128)S(1)} %cholesky.968), custom_call_target="Cholesky" | custom-call | tf_op jit(solution)/shard_map/jit(cholesky)/cholesky | solution.py:34
  923.6 9.8 custom-call.76
  936.5 11.7 %cholesky.883 = f32[128,128]{1,0:T(8,128)S(1)} custom-call(f32[128,128]{1,0:T(8,128)S(1)} %cholesky.973), custom_call_target="Cholesky" | custom-call | tf_op jit(solution)/shard_map/jit(cholesky)/cholesky | solution.py:34
  948.8 9.8 custom-call.77
  961.3 11.7 %cholesky.900 = f32[128,128]{1,0:T(8,128)S(1)} custom-call(f32[128,128]{1,0:T(8,128)S(1)} %convolution_subtract_fusion.40), custom_call_target="Cholesky" | custom-call | tf_op jit(solution)/shard_map/jit(cholesky)/cholesky | solution.py:34
  984.1 4.9 select_select_fusion
  989.0 23.1 %while.9 = (s32[]{:T(128)}, f32[1024,1024]{1,0:T(8,128)}, s32[8,2]{0,1:T(2,128)S(1)}, f32[8,128,128]{2,1,0:T(8,128)S(1)}, s32[]{:T(128)}) while((s32[]{:T(128)}, f32[1024,1024]{1,0:T(8,128)}, s32[8,2]{0,1:T(2,128)S(1)}, f32[8,128,128]{2,1,0:T(8,128)S(1)}, s32[]{:T(128)}) %tuple.205), condition=%wide.while_cond.clone, body=%wide.while_body.clone.sunk | while | flops 2 | bytes 131189 | solution.py:39
  1012.9 79.6 %custom-call.78 = f32[8,128,128]{1,2,0:T(8,128)S(1)} custom-call(f32[8,128,128]{2,1,0:T(8,128)} %copy-done.19), custom_call_target="InvertDiagBlocksLowerTriangular" | custom-call | tf_op jit(solution)/shard_map/jit(_cho_solve)/triangular_solve | solution.py:39
  (456 shorter events, 280.5 us)
Async XLA Ops:
  7.2 77.2 %all-gather.27.cloned.1.call-start = ((), (), s32[]{:S(2)}) async-start(), calls=%async_computation.6 | async-start | bytes 4718592 | tf_op jit(solution)/shard_map/all_gather | solution.py:50
  7.2 26.4 %collective-permute-start = (bf16[2,128,2048]{2,1,0:T(8,128)(2,1)}, bf16[2,128,2048]{2,1,0:T(8,128)(2,1)S(1)}, u32[]{:S(2)}, u32[]{:S(2)}) collective-permute-start(bf16[2,128,2048]{2,1,0:T(8,128)(2,1)} %bitcast.516), channel_id=1, source_target_pairs={{0,8},{8,0},{16,24},{24,16},{1,9},{9,1},{17,25},{25,17},{2,10},{10... | collective-permute-start | bytes 3145736 | tf_op jit(solution)/shard_map/ppermute | solution.py:10
  35.8 492.0 %copy-start.13 = (bf16[128,2048]{1,0:T(8,128)(2,1)}, bf16[128,2048]{1,0:T(8,128)(2,1)S(1)}, u32[]{:S(2)}) copy-start(bf16[128,2048]{1,0:T(8,128)(2,1)S(1)} %get-tuple-element.70) | copy-start | bytes 1572868
  35.9 96.4 %all-gather.29.cloned.1.call-start = ((), (), s32[]{:S(2)}) async-start(), calls=%async_computation.7 | async-start | bytes 4718592 | tf_op jit(solution)/shard_map/all_gather | solution.py:49
  36.8 153.0 %all-gather.15.cloned.1.call-start = ((), (), s32[]{:S(2)}) async-start(), calls=%async_computation | async-start | bytes 4718592 | tf_op jit(solution)/shard_map/all_gather | solution.py:33
  136.8 2.0 copy-start
  143.1 466.8 %all-gather.33.cloned.1.call-start = ((), (), s32[]{:S(2)}) async-start(), calls=%async_computation.9 | async-start | bytes 4718592 | tf_op jit(solution)/shard_map/all_gather | solution.py:49
  143.1 3.3 copy-start.1
  200.1 1.9 copy-start.9
  511.8 5.1 copy-start.5
  524.6 2.8 copy-start.15
  536.6 25.5 %collective-permute-start.1 = (bf16[2,128,2048]{2,1,0:T(8,128)(2,1)S(1)}, bf16[2,128,2048]{2,1,0:T(8,128)(2,1)}, u32[]{:S(2)}, u32[]{:S(2)}) collective-permute-start(bf16[2,128,2048]{2,1,0:T(8,128)(2,1)S(1)} %pad_maximum_fusion), channel_id=1, source_target_pairs={{0,16},{8,24},{16,0},{24,8},{1,17},{9,25},{17,1},{25,9},{2,18},{10... | collective-permute-start | bytes 3145736 | tf_op jit(solution)/shard_map/ppermute | solution.py:10
  564.7 92.4 %all-gather.31.cloned.1.call-start = ((), (), s32[]{:S(2)}) async-start(), calls=%async_computation.8 | async-start | bytes 4718592 | tf_op jit(solution)/shard_map/all_gather | solution.py:50
  565.9 120.6 %all-gather.19.cloned.1.call-start = ((), (), s32[]{:S(2)}) async-start(), calls=%async_computation.2 | async-start | bytes 2359296 | tf_op jit(solution)/shard_map/all_gather | solution.py:52
  566.7 149.9 %all-gather.21.cloned.1.call-start = ((), (), s32[]{:S(2)}) async-start(), calls=%async_computation.3 | async-start | bytes 2359296 | tf_op jit(solution)/shard_map/all_gather | solution.py:51
  567.8 198.3 %all-gather.17.cloned.1.call-start = ((), (), s32[]{:S(2)}) async-start(), calls=%async_computation.1 | async-start | bytes 4718592 | tf_op jit(solution)/shard_map/all_gather | solution.py:33
  661.6 2.0 copy-start.3
  663.6 4.3 copy-start.14
  663.6 5.3 copy-start.20
  667.8 450.2 %all-gather.23.cloned.1.call-start = ((), (), s32[]{:S(2)}) async-start(), calls=%async_computation.4 | async-start | bytes 2359296 | tf_op jit(solution)/shard_map/all_gather | solution.py:52
  668.6 451.5 %all-gather.25.cloned.1.call-start = ((), (), s32[]{:S(2)}) async-start(), calls=%async_computation.5 | async-start | bytes 2359296 | tf_op jit(solution)/shard_map/all_gather | solution.py:51
  668.9 4.3 collective-permute-start.2
  673.3 5.0 collective-permute-start.3
  716.7 6.4 copy-start.4
  720.9 6.4 copy-start.11
  776.4 2.0 copy-start.10
  806.4 0.8 copy-start.12
  1012.1 0.8 copy-start.19
  1092.5 5.1 copy-start.7
  1113.9 3.4 copy-start.8
  1115.5 2.3 copy-start.17
  1115.5 2.3 copy-start.18
  1120.1 4.5 copy-start.2
  1122.3 6.6 copy-start.6
  1131.1 7.1 copy-start.16
Sparse Core Ops, SparseCore 0:
  36.0 48.3 all-gather.26
  86.6 45.6 all-gather.28
  143.2 46.6 all-gather.14
  564.8 45.0 all-gather.32
  611.3 45.6 all-gather.30
  658.5 27.9 all-gather.18
  688.1 28.5 all-gather.20
  718.8 47.1 all-gather.16
  767.7 27.4 all-gather.22
  796.6 28.6 all-gather.24
where the time goes:
time: 1170 us; the launch traced here: 1160 us
  other arithmetic  529 us (45%)
  waiting for transfers between devices  349 us (30%)
  matrix products  163 us (14%)
  local copies, waits for them, and re-layouts  79.1 us (7%)
  between operations  27.1 us (2%)
    another operation x61, other arithmetic, factor_interface(): return (coupling, jnp.linalg.cholesky(gram))  345 us
    another operation x5, other arithmetic, apply_inverse(): return jax.scipy.linalg.cho_solve((triangle, True), moved.T).T  168 us
    all_gather x2, waiting for transfers between devices, exchange_children(): lax.all_gather(right_block[1], 'col', axis=0, tiled=True)  94.7 us
    all_gather x2, waiting for transfers between devices, exchange_children(): lax.all_gather(left_block[1], 'col', axis=0, tiled=True)  89.9 us
    all_gather x2, waiting for transfers between devices, factor_interface(): gram = lax.all_gather(own_gram, 'col', axis=0, tiled=True)  75.3 us
    ppermute x4, waiting for transfers between devices, partner_2(): return lax.ppermute(value, axis, pairs)  53.6 us
    another operation x120, matrix products, apply_inverse(): return jax.scipy.linalg.cho_solve((triangle, True), moved.T).T  47.3 us
    another operation x28, matrix products, factor_interface(): return (coupling, jnp.linalg.cholesky(gram))  47.2 us
  transfers between devices with their start and end apart: 14, of which 12 were waited for; matrix products, arithmetic and copies ran while one was open for 33% of the time, Pallas kernels for 0%

commit v1 on v0

v1 whole, which is shorter than its diff:
```python
import functools
import jax
import jax.numpy as jnp
from jax import lax
from jax.experimental import pallas as pl
from jax.experimental.pallas import tpu as pltpu
from jax.sharding import Mesh, PartitionSpec as P

BF = jnp.bfloat16
F32 = jnp.float32
VMEM_LIMIT = 60 * 1024 * 1024
SMALL_POWER = 36.0
LAST_POWER = 1e12
MAX_SQUARINGS = 10
TARGET = 3e-5
MAX_STEPS = 12
MAX_NEWTON = 80


def mul(left, right):
    return jnp.dot(left, right, preferred_element_type=F32)


def mul_full(left, right):
    return jnp.dot(left, right, preferred_element_type=F32, precision=lax.Precision.HIGHEST)


def fold(values):
    rows, columns = values.shape
    return jnp.sum((values * values).reshape(rows // 8, 8, columns), axis=0)


def eye_block(start, rows, columns):
    row = lax.broadcasted_iota(jnp.int32, (rows, columns), 0) + start
    column = lax.broadcasted_iota(jnp.int32, (rows, columns), 1)
    return (row == column).astype(F32)


def factor_kernel(left, right, g_hi, g_lo, inverse, good, powers):
    middle = left.shape[0]
    block = min(256, middle)
    count = middle // block
    nothing = jnp.zeros((8, middle), F32)

    def first(index, total):
        rows = pl.ds(pl.multiple_of(index * block, block), block)
        product = mul(right[rows, :], left[...])
        high = product.astype(BF)
        g_hi[rows, :] = high
        powers[0, rows, :] = high
        g_lo[rows, :] = (product - high.astype(F32)).astype(BF)
        inverse[rows, :] = (product + eye_block(index * block, block, middle)).astype(BF)
        return total + fold(product)

    size = jnp.sum(lax.fori_loop(0, count, first, nothing))

    def more(state):
        step, size = state
        return (step < MAX_SQUARINGS) & (size >= SMALL_POWER) & (size < LAST_POWER)

    def double(state):
        step, _ = state
        now = lax.rem(step, 2)
        later = 1 - now

        def square(index, total):
            rows = pl.ds(pl.multiple_of(index * block, block), block)
            product = mul(powers[now, rows, :], powers[now])
            powers[later, rows, :] = product.astype(BF)
            return total + fold(product)

        size = jnp.sum(lax.fori_loop(0, count, square, nothing))

        def extend(index, carry):
            rows = pl.ds(pl.multiple_of(index * block, block), block)
            held = inverse[rows, :]
            inverse[rows, :] = (held.astype(F32) + mul(held, powers[later])).astype(BF)
            return carry

        lax.fori_loop(0, count, extend, 0)
        return (step + 1, size)

    _, size = lax.while_loop(more, double, (0, size))
    good[0] = (size < SMALL_POWER).astype(jnp.int32)


def factor(left, right):
    middle = left.shape[0]
    whole = jax.ShapeDtypeStruct((middle, middle), BF)
    inside = pl.BlockSpec(memory_space=pltpu.VMEM)
    return pl.pallas_call(
        factor_kernel,
        name="factor",
        out_shape=(whole, whole, whole, jax.ShapeDtypeStruct((1,), jnp.int32)),
        in_specs=[inside, inside],
        out_specs=(inside, inside, inside, pl.BlockSpec(memory_space=pltpu.SMEM)),
        scratch_shapes=[pltpu.VMEM((2, middle, middle), BF)],
        compiler_params=pltpu.CompilerParams(vmem_limit_bytes=VMEM_LIMIT),
    )(left, right)


def row_sums(values):
    return jnp.sum(values * values, axis=1, keepdims=True)


def refine(rhs, answer, g_hi, g_lo, inverse, good):
    answer[...] = mul(rhs[...].astype(BF), inverse[...])
    base = row_sums(rhs[...])
    base = jnp.where(base > 0, base, 1.0)

    def more(state):
        step, _, going = state
        return going == 1

    def correct(state):
        step, before, _ = state
        held = answer[...]
        high = held.astype(BF)
        low = (held - high.astype(F32)).astype(BF)
        rest = rhs[...] - held + mul(high, g_hi[...]) + (mul(low, g_hi[...]) + mul(high, g_lo[...]))
        answer[...] = held + mul(rest.astype(BF), inverse[...])
        now = jnp.max(row_sums(rest) / base)
        done = now * now <= (TARGET * TARGET) * before
        fails = jnp.logical_not(now < 0.25 * before) | (step >= MAX_STEPS)
        going = jnp.where(done, 0, jnp.where(fails, 2, 1)).astype(jnp.int32)
        return (step + 1, now, going)

    start = jnp.where(good[0] == 1, 1, 2).astype(jnp.int32)
    _, _, end = lax.while_loop(more, correct, (0, jnp.float32(1.0), start))
    return end


def general_solve(rhs, answer, left, right, square, rest, held):
    middle = left.shape[0]
    block = min(128, middle)
    wide = min(256, middle)
    count = middle // block

    def rows_of(index):
        return pl.ds(pl.multiple_of(index * block, block), block)

    def columns_of(index):
        return pl.ds(pl.multiple_of(index * wide, wide), wide)

    def build(index, total):
        rows = rows_of(index)
        values = eye_block(index * block, block, middle) - mul(right[rows, :], left[...])
        square[rows, :] = values
        size = jnp.abs(values)
        return (
            total[0] + jnp.sum(size, axis=0, keepdims=True),
            jnp.maximum(total[1], jnp.max(jnp.sum(size, axis=1, keepdims=True))),
        )

    column_total, row_most = lax.fori_loop(
        0, count, build, (jnp.zeros((1, middle), F32), jnp.float32(0.0))
    )
    scale = 1.0 / (jnp.max(column_total) * row_most)

    def turn(index, carry):
        row = pl.multiple_of(lax.div(index, count) * block, block)
        column = pl.multiple_of(lax.rem(index, count) * block, block)
        piece = square[pl.ds(row, block), pl.ds(column, block)]
        held[0, pl.ds(column, block), pl.ds(row, block)] = piece.T * scale
        return carry

    lax.fori_loop(0, count * count, turn, 0)
    wides = middle // wide

    def newton(state):
        step, _, before, _ = state
        now = lax.rem(step, 2)

        def residual(index, total):
            row = pl.multiple_of(lax.div(index, wides) * block, block)
            column = pl.multiple_of(lax.rem(index, wides) * wide, wide)
            rows, columns = pl.ds(row, block), pl.ds(column, wide)
            row_id = lax.broadcasted_iota(jnp.int32, (block, wide), 0) + row
            column_id = lax.broadcasted_iota(jnp.int32, (block, wide), 1) + column
            values = (row_id == column_id).astype(F32) - mul_full(
                held[now, rows, :], square[:, columns]
            )
            rest[rows, columns] = values
            return total + fold(values)

        size = jnp.sum(lax.fori_loop(0, count * wides, residual, jnp.zeros((8, wide), F32)))

        def update(index, carry):
            row = pl.multiple_of(lax.div(index, wides) * block, block)
            column = pl.multiple_of(lax.rem(index, wides) * wide, wide)
            rows, columns = pl.ds(row, block), pl.ds(column, wide)
            held[1 - now, rows, columns] = held[now, rows, columns] + mul_full(
                rest[rows, :], held[now, :, columns]
            )
            return carry

        lax.fori_loop(0, count * wides, update, 0)
        near = (size < 1e-5) | ((size < 0.1) & (size > 0.5 * before))
        return (step + 1, 1 - now, size, near.astype(jnp.int32))

    def more(state):
        step, _, _, near = state
        return (near == 0) & (step < MAX_NEWTON)

    _, now, _, _ = lax.while_loop(more, newton, (0, 0, jnp.float32(jnp.inf), 0))

    def by_columns(index, carry):
        columns = columns_of(index)
        answer[:, columns] = mul_full(rhs[...], held[now, :, columns])
        return carry

    lax.fori_loop(0, wides, by_columns, 0)
    count_rows = rhs.shape[0]

    def again(step, carry):
        def left_over(index, carry):
            columns = columns_of(index)
            rest[:count_rows, columns] = rhs[:, columns] - mul_full(answer[...], square[:, columns])
            return carry

        lax.fori_loop(0, wides, left_over, 0)

        def add(index, carry):
            columns = columns_of(index)
            answer[:, columns] += mul_full(rest[:count_rows, :], held[now, :, columns])
            return carry

        lax.fori_loop(0, wides, add, 0)
        return carry

    lax.fori_loop(0, 2, again, 0)


def apply_kernel(own, down, *refs):
    inputs = 6 + (2 if own else 0) + (3 if down else 0)
    outputs = (2 if own else 0) + (2 if down else 0)
    g_hi, g_lo, inverse, good, left, right = refs[:6]
    own_refs = refs[6:8] if own else ()
    down_refs = refs[inputs - 3 : inputs] if down else ()
    out_refs = refs[inputs : inputs + outputs]
    rhs, answer, through, square, rest, held = refs[inputs + outputs :]
    middle = left.shape[0]
    if own:
        left_own, right_own = own_refs
        rhs[:own, :] = left_own[...].astype(F32)
        rhs[own : 2 * own, :] = mul(right_own[...], left[...])
    if down:
        left_io, right_io, loads = down_refs
        passed = mul(loads[:, middle:].astype(BF), right_io[...])
        through[...] = passed
        rhs[2 * own :, :] = mul(loads[:, :middle].astype(BF), left_io[...]) + mul(
            passed.astype(BF), left[...]
        )
    end = refine(rhs, answer, g_hi, g_lo, inverse, good)

    @pl.when(end != 0)
    def _():
        general_solve(rhs, answer, left, right, square, rest, held)

    solved = answer[...].astype(BF)
    carried = mul(solved, right[...])
    if own:
        out_refs[0][...] = solved[: 2 * own]
        out_refs[1][:own, :] = carried[:own].astype(BF)
        out_refs[1][own:, :] = (right_own[...].astype(F32) + carried[own : 2 * own]).astype(BF)
    if down:
        out_refs[-2][...] = answer[2 * own :, :]
        out_refs[-1][...] = through[...] + carried[2 * own :]


def apply(factors, left, right, own_rows, down_rows):
    middle = left.shape[0]
    own = own_rows[0].shape[0] if own_rows else 0
    down = down_rows[2].shape[0] if down_rows else 0
    total = 2 * own + down
    inside = pl.BlockSpec(memory_space=pltpu.VMEM)
    out_shape = ()
    if own:
        out_shape += (jax.ShapeDtypeStruct((2 * own, middle), BF),) * 2
    if down:
        out_shape += (jax.ShapeDtypeStruct((down, middle), F32),) * 2
    arguments = (*factors, left, right, *own_rows, *down_rows)
    in_specs = [inside] * len(arguments)
    in_specs[3] = pl.BlockSpec(memory_space=pltpu.SMEM)
    return pl.pallas_call(
        functools.partial(apply_kernel, own, down),
        name="apply",
        out_shape=out_shape,
        in_specs=in_specs,
        out_specs=(inside,) * len(out_shape),
        scratch_shapes=[
            pltpu.VMEM((total, middle), F32),
            pltpu.VMEM((total, middle), F32),
            pltpu.VMEM((max(down, 8), middle), F32),
            pltpu.VMEM((middle, middle), F32),
            pltpu.VMEM((middle, middle), F32),
            pltpu.VMEM((2, middle, middle), F32),
        ],
        compiler_params=pltpu.CompilerParams(vmem_limit_bytes=VMEM_LIMIT),
    )(*arguments)


def gather(value, axes):
    return lax.all_gather(value, axes, axis=0, tiled=True)


def per_device(box_maps, group_loads):
    block = box_maps[0]
    own, ports = block.shape[1], block.shape[2]
    middle = ports // 2
    half = middle // 2
    low = lax.axis_index("lo")
    high = lax.axis_index("hi")
    position = lax.axis_index("col")
    is_left = low == 0
    pair = ("lo", "col")
    group = ("hi", "lo", "col")

    faces = gather(block[1][:, middle:], pair)
    left_ii, right_ii = faces[:middle], faces[middle:]
    mine = low * half
    other = half - mine

    def cut(side, start):
        return lax.dynamic_slice_in_dim(block[side], start, half, 1)

    cross = block[0][:, middle:]
    kept = jnp.concatenate([cut(0, mine), cross, cut(1, mine)], axis=1)
    sent = jnp.concatenate([cut(0, other), cross, cut(1, other)], axis=1)
    received = lax.ppermute(sent, "lo", [(0, 1), (1, 0)])
    left_all = jnp.where(is_left, kept, received)
    right_all = jnp.where(is_left, received, kept)
    outer = jnp.concatenate([left_all[:, half + middle :], right_all[:, half + middle :]], axis=1)
    outer = gather(outer, "col")
    loads = gather(group_loads[0], ("hi", "lo"))

    factors = factor(left_ii, right_ii)
    solved, carried = apply(
        factors,
        left_ii,
        right_ii,
        (left_all[:, half : half + middle], right_all[:, half : half + middle]),
        (),
    )
    upper = mul(carried, outer[:, :half])
    lower = mul(solved, outer[:, half:])
    upper_left = (left_all[:, :half].astype(F32) + upper[:own]).astype(BF)
    upper_right = upper[own:].astype(BF)
    lower_left = lower[:own].astype(BF)
    lower_right = (right_all[:, :half].astype(F32) + lower[own:]).astype(BF)

    def joined(value):
        whole = gather(value, group).reshape(2, 2, middle, half)
        return (
            jnp.concatenate([whole[0, 0], whole[0, 1]], axis=1),
            jnp.concatenate([whole[1, 0], whole[1, 1]], axis=1),
        )

    pair_left_ii, pair_right_ii = joined(lower_right)
    pair_left_io, pair_right_io = joined(lower_left)
    pair_outer = gather(upper_right, "col")
    cross_all = gather(cross, pair)

    pair_factors = factor(pair_left_ii, pair_right_ii)

    def own_rows(value):
        return lax.dynamic_slice_in_dim(value, position * own, own, 0)

    solved_two, carried_two, x_left, x_right = apply(
        pair_factors,
        pair_left_ii,
        pair_right_ii,
        (own_rows(pair_left_io), own_rows(pair_right_io)),
        (pair_left_io, pair_right_io, loads),
    )
    is_upper = high == 0
    top = mul(jnp.where(is_upper, carried_two, solved_two), pair_outer)
    outer_own = upper_left.astype(F32)
    nothing = jnp.zeros_like(outer_own)
    top = top + jnp.concatenate(
        [jnp.where(is_upper, outer_own, nothing), jnp.where(is_upper, nothing, outer_own)], axis=0
    )
    top_block = top.reshape(1, 2, own, half)

    first = jnp.where(is_upper, loads[:, :middle], loads[:, middle:])
    second = jnp.where(is_upper, x_right, x_left)
    pair_loads = jnp.concatenate([first, second], axis=1)
    y_left, y_right = apply(
        factors, left_ii, right_ii, (), (cross_all[:middle], cross_all[middle:], pair_loads)
    )
    leaf = jnp.concatenate(
        [jnp.where(is_left, first, second), jnp.where(is_left, y_right, y_left)], axis=1
    )
    return (top_block, leaf[None])


def solution(mesh):
    boxes, columns = mesh.devices.shape
    split = Mesh(mesh.devices.reshape(boxes // 4, 2, 2, columns), ("group", "hi", "lo", "col"))
    box = ("group", "hi", "lo")
    placed = (P(box, None, "col", None), P(box, "col", None))
    return jax.shard_map(
        per_device,
        mesh=split,
        in_specs=placed,
        out_specs=placed,
        check_vma=False,
    )
```

time: 1170 us -> 1260 us (1.077)
  waiting for transfers between devices: 349 us -> 1040 us
  other arithmetic: 529 us -> 13.7 us
  matrix products: 163 us -> 6 us
  Pallas kernels: 0 us -> 155 us
  local copies, waits for them, and re-layouts: 79.1 us -> 19.3 us
  between operations: 27.1 us -> 14.3 us
    all_gather x10 -> x6, waiting for transfers between devices: 295 us -> 1020 us  [gather(): return lax.all_gather(value, axes, axis=0, tiled=True)]
    another operation x72 -> x0, other arithmetic: 514 us -> none  [the longest x61 345 us: factor_interface(): return (coupling, jnp.linalg.cholesky(gram))]
    pallas_call x0 -> x5, Pallas kernels: none -> 155 us  [the longest x2 98.8 us: factor(): pl.pallas_call(factor_kernel, name='factor', out_shape=(whole, whole, who...]
    another operation x148 -> x0, matrix products: 94.6 us -> none  [the longest x120 47.3 us: apply_inverse(): return jax.scipy.linalg.cho_solve((triangle, True), moved.T).T]
    dot_general x26 -> x3, matrix products: 68.6 us -> 6 us  [mul(): return jnp.dot(left, right, preferred_element_type=F32)]
    another operation x83 -> x0, local copies, waits for them, and re-layouts: 51.3 us -> none  [the longest x67 46.2 us: apply_inverse(): return jax.scipy.linalg.cho_solve((triangle, True), moved.T).T]
    ppermute x4 -> x1, waiting for transfers between devices: 53.6 us -> 14 us  [per_device(): received = lax.ppermute(sent, 'lo', [(0, 1), (1, 0)])]
  transfers between devices with their start and end apart: 14 -> 7, of which waited for: 12 -> 4; matrix products, arithmetic and copies ran while one was open for 33% -> 3% of each run, Pallas kernels for 0% -> 12%
where the time goes in v1:
time: 1260 us
  waiting for transfers between devices  1040 us (83%)
  Pallas kernels  155 us (12%)
  local copies, waits for them, and re-layouts  19.3 us (2%)
  between operations  14.3 us (1%)
  other arithmetic  13.7 us (1%)
    all_gather x6, waiting for transfers between devices, gather(): return lax.all_gather(value, axes, axis=0, tiled=True)  1020 us
    pallas_call x2, Pallas kernels, factor(): pl.pallas_call(factor_kernel, name='factor', out_shape=(whole, whole, who...  98.8 us
    pallas_call x3, Pallas kernels, apply(): pl.pallas_call(functools.partial(apply_kernel, own, down), name='apply',...  55.7 us
  transfers between devices with their start and end apart: 7, of which 4 were waited for; matrix products, arithmetic and copies ran while one was open for 3% of the time, Pallas kernels for 12%

profile of v1, /device:TPU:0, one launch (start us, length us, event | category | flops | bytes accessed | tf_op | source)
XLA Modules:
  0.0 1257.6 jit_solution(359336744615404426)
XLA Ops:
  7.2 0.0 all-gather.8.cloned.1.call-start
  7.2 1.4 fusion.14
  8.6 0.7 slice.130
  9.4 0.0 all-gather.8.cloned.1.call-update
  9.4 0.0 all-gather.10.cloned.1.call-start
  9.6 3.0 collective-permute-start
  12.6 14.0 %collective-permute-done = bf16[128,2048]{1,0:T(8,128)(2,1)S(1)} collective-permute-done((bf16[128,2048]{1,0:T(8,128)(2,1)S(1)}, bf16[128,2048]{1,0:T(8,128)(2,1)S(1)}, u32[]{:S(2)}, u32[]{:S(2)}) %collective-permute-start) | collective-permute-done | bytes 524320 | tf_op jit(solution)/shard_map/ppermute | solution.py:330
  26.6 0.2 broadcast_select_fusion.1
  26.9 0.8 pad_maximum_fusion.7
  27.7 0.0 all-gather.18.cloned.1.call-start
  27.7 0.7 all-gather.18.cloned.1.call-update
  28.4 0.0 all-gather.12.cloned.1.call-start
  28.4 0.7 slice.133.refs_6_
  29.2 0.7 slice.134.refs_7_
  29.9 35.3 %all-gather.8.cloned.1.call-done = bf16[2048,1024]{1,0:T(8,128)(2,1)} async-done(((bf16[128,1024]{1,0:T(8,128)(2,1)}), bf16[2048,1024]{1,0:T(8,128)(2,1)}) %all-gather.8.cloned.1.call-update) | async-done | bytes 4194320 | tf_op jit(solution)/shard_map/all_gather | solution.py:304
  65.2 4.6 fusion.13
  69.8 49.4 %factor.2 = (bf16[1024,1024]{1,0:T(8,128)(2,1)}, bf16[1024,1024]{1,0:T(8,128)(2,1)}, bf16[1024,1024]{1,0:T(8,128)(2,1)}, s32[1]{0:T(128)}) custom-call(bf16[1024,1024]{1,0:T(8,128)(2,1)} %get-tuple-element.48.left.refs_4_, bf16[1024,1024]{1,0:T(8,128)(2,1)} %get-tuple-element.47.right.refs_5_), custom_call_target="tpu_custom_call" | custom-call | tf_op jit(solution)/shard_map/factor/pallas_call | solution.py:91
  119.2 19.8 %apply.3 = (bf16[256,1024]{1,0:T(8,128)(2,1)}, bf16[256,1024]{1,0:T(8,128)(2,1)}) custom-call(bf16[1024,1024]{1,0:T(8,128)(2,1)} %get-tuple-element.18.refs_0_, bf16[1024,1024]{1,0:T(8,128)(2,1)} %get-tuple-element.19.refs_1_, bf16[1024,1024]{1,0:T(8,128)(2,1)} %get-tuple-element.20.refs_2_, s32[1]{0:T(128)} %get-tuple-element.21.refs_3_, ...), custom_call_target="tpu_custom_call" | custom-call | tf_op jit(solution)/shard_map/apply/pallas_call | solution.py:285
  139.0 1.9 fusion.2
  140.9 0.7 fusion.11
  141.6 0.0 all-gather.14.cloned.1.call-start
  141.7 0.7 slice.191
  142.4 0.0 all-gather.16.cloned.1.call-start
  142.4 10.7 all-gather
  153.1 1.7 fusion
  154.8 0.7 slice.190
  155.5 0.1 convert_select_fusion.1
  155.5 0.0 all-gather.16.cloned.1.call-update
  155.6 0.0 all-gather.18.cloned.1.call-done
  155.6 4.7 fusion.12
  160.3 977.6 %all-gather.12.cloned.1.call-done = bf16[4096,512]{1,0:T(8,128)(2,1)} async-done(((bf16[128,512]{1,0:T(8,128)(2,1)}), bf16[4096,512]{1,0:T(8,128)(2,1)}) %all-gather.12.cloned.1.call-update) | async-done | bytes 4194320 | tf_op jit(solution)/shard_map/all_gather | solution.py:304
  1138.0 2.4 slice_bitcast_fusion.5
  1140.4 1.7 pad_maximum_fusion.3.right.refs_5_
  1142.1 1.7 pad_maximum_fusion.2.left.refs_4_
  1143.8 49.4 %factor.3 = (bf16[1024,1024]{1,0:T(8,128)(2,1)}, bf16[1024,1024]{1,0:T(8,128)(2,1)}, bf16[1024,1024]{1,0:T(8,128)(2,1)}, s32[1]{0:T(128)}) custom-call(bf16[1024,1024]{1,0:T(8,128)(2,1)} %pad_maximum_fusion.2.left.refs_4_, bf16[1024,1024]{1,0:T(8,128)(2,1)} %pad_maximum_fusion.3.right.refs_5_), custom_call_target="tpu_custom_call" | custom-call | tf_op jit(solution)/shard_map/factor/pallas_call | solution.py:91
  1193.2 8.1 all-gather.14.cloned.1.call-done
  1201.3 2.4 slice_bitcast_fusion
  1203.8 0.7 fusion.8.refs_7_
  1204.5 0.7 fusion.9.refs_6_
  1205.3 1.7 pad_maximum_fusion.1.refs_9_
  1207.0 1.7 pad_maximum_fusion.refs_8_
  1208.7 19.2 %apply.4 = (bf16[256,1024]{1,0:T(8,128)(2,1)}, bf16[256,1024]{1,0:T(8,128)(2,1)}, f32[64,1024]{1,0:T(8,128)}, f32[64,1024]{1,0:T(8,128)}) custom-call(bf16[1024,1024]{1,0:T(8,128)(2,1)} %get-tuple-element.23.refs_0_, bf16[1024,1024]{1,0:T(8,128)(2,1)} %get-tuple-element.24.refs_1_, bf16[1024,1024]{1,0:T(8,128)(2,1)} %get-tuple-element.25.refs_2_, ...), custom_call_target="tpu_custom_call" | custom-call | tf_op jit(solution)/shard_map/apply/pallas_call | solution.py:285
  1227.9 1.0 broadcast_select_fusion.4
  1229.0 0.8 pad_maximum_fusion.6.refs_8_
  1229.8 16.7 %apply.5 = (f32[64,1024]{1,0:T(8,128)}, f32[64,1024]{1,0:T(8,128)}) custom-call(bf16[1024,1024]{1,0:T(8,128)(2,1)} %get-tuple-element.18.refs_0_, bf16[1024,1024]{1,0:T(8,128)(2,1)} %get-tuple-element.19.refs_1_, bf16[1024,1024]{1,0:T(8,128)(2,1)} %get-tuple-element.20.refs_2_, s32[1]{0:T(128)} %get-tuple-element.21.refs_3_, ...), custom_call_target="tpu_custom_call" | custom-call | tf_op jit(solution)/shard_map/apply/pallas_call | solution.py:285
  1246.5 1.0 broadcast_select_fusion.3
  1247.5 0.8 maximum_bitcast_fusion
  1248.3 2.5 convolution_add_fusion
  (22 shorter events, 0.2 us)
Async XLA Ops:
  7.2 58.0 %all-gather.8.cloned.1.call-start = ((), (), s32[]{:S(2)}) async-start(), calls=%async_computation | async-start | bytes 4456448 | tf_op jit(solution)/shard_map/all_gather | solution.py:304
  9.4 129.6 %all-gather.10.cloned.1.call-start = ((), (), s32[]{:S(2)}) async-start(), calls=%async_computation.1 | async-start | bytes 2359296 | tf_op jit(solution)/shard_map/all_gather | solution.py:304
  9.5 17.4 %copy-start.1 = (bf16[128,1024]{1,0:T(8,128)(2,1)}, bf16[128,1024]{1,0:T(8,128)(2,1)S(1)}, u32[]{:S(2)}) copy-start(bf16[128,1024]{1,0:T(8,128)(2,1)S(1)} %slice.128) | copy-start | bytes 786436
  9.6 17.0 %collective-permute-start = (bf16[128,2048]{1,0:T(8,128)(2,1)S(1)}, bf16[128,2048]{1,0:T(8,128)(2,1)S(1)}, u32[]{:S(2)}, u32[]{:S(2)}) collective-permute-start(bf16[128,2048]{1,0:T(8,128)(2,1)S(1)} %fusion.4), channel_id=1, source_target_pairs={{0,8},{8,0},{1,9},{9,1},{2,10},{10,2},{3,11},{11,3},{4,12},{12,4},... | collective-permute-start | bytes 1572872 | tf_op jit(solution)/shard_map/ppermute | solution.py:330
  27.7 127.9 %all-gather.18.cloned.1.call-start = ((), (), s32[]{:S(2)}) async-start(), calls=%async_computation.5 | async-start | bytes 4456448 | tf_op jit(solution)/shard_map/all_gather | solution.py:304
  28.4 1109.6 %all-gather.12.cloned.1.call-start = ((), (), s32[]{:S(2)}) async-start(), calls=%async_computation.2 | async-start | bytes 4325376 | tf_op jit(solution)/shard_map/all_gather | solution.py:304
  139.0 3.4 copy-start.4
  139.0 14.2 %copy-start.5 = (bf16[256,1024]{1,0:T(8,128)(2,1)S(1)}, bf16[256,1024]{1,0:T(8,128)(2,1)}, u32[]{:S(2)}) copy-start(bf16[256,1024]{1,0:T(8,128)(2,1)} %get-tuple-element.29) | copy-start | bytes 1572868
  141.6 1059.7 %all-gather.14.cloned.1.call-start = ((), (), s32[]{:S(2)}) async-start(), calls=%async_computation.3 | async-start | bytes 4325376 | tf_op jit(solution)/shard_map/all_gather | solution.py:304
  142.4 1105.9 %all-gather.16.cloned.1.call-start = ((), (), s32[]{:S(2)}) async-start(), calls=%async_computation.4 | async-start | bytes 1179648 | tf_op jit(solution)/shard_map/all_gather | solution.py:304
  1208.7 19.3 %copy-start = (f32[1,64,2048]{2,1,0:T(8,128)S(1)}, f32[1,64,2048]{2,1,0:T(8,128)}, u32[]{:S(2)}) copy-start(f32[1,64,2048]{2,1,0:T(8,128)} %all-gather) | copy-start | bytes 1572868
  1229.8 18.5 %copy-start.2 = (bf16[256,1024]{1,0:T(8,128)(2,1)S(1)}, bf16[256,1024]{1,0:T(8,128)(2,1)}, u32[]{:S(2)}) copy-start(bf16[256,1024]{1,0:T(8,128)(2,1)} %get-tuple-element.28) | copy-start | bytes 1572868
  1229.8 18.5 %copy-start.3 = (bf16[256,1024]{1,0:T(8,128)(2,1)S(1)}, bf16[256,1024]{1,0:T(8,128)(2,1)}, u32[]{:S(2)}) copy-start(bf16[256,1024]{1,0:T(8,128)(2,1)} %get-tuple-element.27) | copy-start | bytes 1572868
Sparse Core Ops, SparseCore 0:
  10.7 54.3 all-gather.7
  66.8 27.6 all-gather.9
  96.7 49.7 all-gather.17
  149.9 988.0 all-gather.11
  1140.8 60.4 all-gather.13
  1202.8 21.0 all-gather.15
